TPU v7x, 256 devices: a whole 4x4x8 slice. The times are simulated.
256 devices in a mesh: pix: 64 (over x, z, core), band: 4 (over y).
Axes of the slice: x: 4, y: 4, z: 8, core: 2. Of those that a mesh axis runs over, the one named last changes fastest.
Arguments:
- spectra: bfloat16 [224, 262144], P('band', 'pix'), may hold values from -0.1 to 4
- endmembers: bfloat16 [224, 512], P('band'), may hold values from 0.05 to 1
- gram_inverse: float32 [512, 512], replicated, may hold values from -1 to 1, as said below
- abundances: float32 [512, 262144], P(None, ('pix', 'band')), may hold values from 0 to 512, as said below
- duals: float32 [512, 262144], P(None, ('pix', 'band')), may hold values from -4 to 4
Outputs:
- abundances_out: float32 [512, 262144], P(None, ('pix', 'band'))
- duals_out: float32 [512, 262144], P(None, ('pix', 'band'))
- residual_rms: float32 [2, 2], replicated
Inputs may be any that keep to these rules, and one draw needn't show every extreme that they name: `abundances`: each column is nonnegative and sums to 512. `gram_inverse`: penalty times the float32 inverse of endmembers^T endmembers / 512^2 + penalty I, with penalty = 224 / (2 * 512^2) and the endmembers as stored.
All inputs are finite; a program needn't handle non-finite values.
Results may differ from a plain program's by a relative error of at most 0.0004.
Values may be sent and summed in bfloat16 or wider, within the bound.
A program may use at most 64 MiB of HBM per device.

v0:
```python
import jax
import jax.numpy as jnp
from jax import lax
from jax.sharding import Mesh
from jax.sharding import PartitionSpec as P

B = 224
K = 512
ITERS = 2
BISECT = 6
PIX = ("pix_0", "pix_1", "pix_2")
PIX_BAND = ("pix_0", "pix_1", "pix_2", "band")


def one_axis_at_a_time(shard, axes):
    for axis in axes:
        shard = lax.psum(shard, axis)
    return shard


def project(shifted):
    simplex_sum = float(K)
    high_end = jnp.max(shifted, axis=0)
    low_end = (jnp.sum(shifted, axis=0) - simplex_sum) / simplex_sum

    def mass_at(level):
        return jnp.sum(jnp.maximum(shifted - level[None, :], 0.0), axis=0)

    mass_low = mass_at(low_end)
    mass_high = jnp.zeros_like(high_end)

    def bisect_once(unused, state):
        low_now, high_now, low_mass, high_mass = state
        middle = 0.5 * (low_now + high_now)
        total_mass = mass_at(middle)
        too_high = total_mass > simplex_sum
        return (
            jnp.where(too_high, middle, low_now),
            jnp.where(too_high, high_now, middle),
            jnp.where(too_high, total_mass, low_mass),
            jnp.where(too_high, high_mass, total_mass),
        )

    low_end, high_end, mass_low, mass_high = lax.fori_loop(
        0, BISECT, bisect_once, (low_end, high_end, mass_low, mass_high)
    )
    level = low_end + (mass_low - simplex_sum) * (high_end - low_end) / (mass_low - mass_high)
    return jnp.maximum(shifted - level[None, :], 0.0)


def contract_bands(signatures, columns):
    return lax.dot_general(
        signatures, columns, (((0,), (0,)), ((), ())), preferred_element_type=jnp.float32
    )


def body(spectra, endmembers, gram_inverse, abundances, duals):
    penalty = B / (2.0 * K * K)
    exchanged = lax.all_to_all(spectra, "band", split_axis=1, concat_axis=0, tiled=True)
    all_rows = lax.all_gather(endmembers, "band", axis=0, tiled=True)
    fit_term = contract_bands(all_rows, exchanged)
    fit_term = fit_term / K
    pixel_count = abundances.shape[1] * lax.axis_size(PIX) * lax.axis_size("band")
    current = abundances
    scaled_dual = duals
    primal_list = []
    change_list = []
    for sweep in range(ITERS):
        primal = jnp.dot(
            gram_inverse,
            fit_term / penalty + current - scaled_dual,
            precision=lax.Precision.HIGHEST,
        )
        updated = project(primal + scaled_dual)
        scaled_dual = scaled_dual + primal - updated
        primal_sum = jnp.sum((primal - updated) ** 2)
        change_sum = jnp.sum((updated - current) ** 2)
        primal_list.append(primal_sum)
        change_list.append(change_sum)
        current = updated
    totals = jnp.stack([jnp.stack(primal_list), jnp.stack(change_list)])
    totals = one_axis_at_a_time(totals, PIX_BAND)
    residual_rms = jnp.sqrt(totals / pixel_count)
    return (current, scaled_dual, residual_rms)


def solution(mesh):
    finer = Mesh(
        mesh.devices.reshape(4, 8, 2, mesh.shape["band"]), ("pix_0", "pix_1", "pix_2", "band")
    )
    return jax.shard_map(
        body,
        mesh=finer,
        in_specs=(P("band", PIX), P("band", None), P(), P(None, PIX_BAND), P(None, PIX_BAND)),
        out_specs=(P(None, PIX_BAND), P(None, PIX_BAND), P()),
        check_vma=False,
    )
```

profile of v0, /device:TPU:1, one launch (start us, length us, event | category | flops | bytes accessed | tf_op | source)
XLA Modules:
  0.0 109.2 jit_solution(441457199507730125)
XLA Ops:
  0.6 0.0 copy-start
  0.6 1.9 %copy.12 = bf16[7,4,8,1024]{3,2,0,1:T(8,128)(2,1)} copy(bf16[7,4,8,1024]{3,2,1,0:T(8,128)(2,1)} %bitcast.36) | data formatting | bytes 917504 | tf_op jit(solution)/shard_map/all_to_all | solution.py:59
  2.5 5.0 %all-to-all-start = ((bf16[56,4,1024]{2,0,1:T(8,128)(2,1)}), bf16[56,4,1024]{2,0,1:T(8,128)(2,1)S(1)}, u32[]{:S(2)}, u32[]{:S(2)}) async-start(bf16[56,4,1024]{2,0,1:T(8,128)(2,1)} %bitcast.34), calls=%async_computation | async-start | bytes 917504 | tf_op jit(solution)/shard_map/all_to_all | solution.py:59
  7.6 12.5 %all_gather.3 = bf16[224,512]{1,0:T(8,128)(2,1)S(1)} all-gather(bf16[56,512]{1,0:T(8,128)(2,1)} %param.10), channel_id=1, replica_groups=mesh['pix_0'=4,'pix_1'=8,'pix_2'=2,'band'=4] {'band'}, dimensions={0}, use_global_device_ids=true | all-gather | bytes 286720 | tf_op jit(solution)/shard_map/all_gather | solution.py:60
  20.0 0.0 all-to-all-done
  20.0 0.5 fusion.29
  20.5 0.0 copy-done
  20.5 0.0 copy-start.2
  20.5 8.7 %fusion.28 = (f32[1024]{0:T(1024)S(1)}, f32[512,1024]{1,0:T(8,128)S(1)}, f32[1024,512]{0,1:T(8,128)}) fusion(f32[512,1024]{1,0:T(8,128)} %param.13, f32[512,512]{1,0:T(8,128)S(1)} %copy-done, f32[512,1024]{1,0:T(8,128)} %param.12, f32[512,1024]{1,0:T(8,128)S(1)} %fusion.29), kind=kOutput, calls=%fused_computation.54 | convolution fusion | flops 3223845888 | bytes 11538432 | tf_op jit(solution)/shard_map/dot_general | solution.py:69
  29.2 0.0 copy-done.2
  29.2 0.3 maximum_reduce_fusion.3
  29.5 1.9 %while.34 = (s32[]{:T(128)}, f32[1024]{0:T(1024)S(1)}, f32[1024]{0:T(1024)S(1)}, f32[1024]{0:T(1024)S(1)}, f32[1024]{0:T(1024)S(1)}, /*index=5*/f32[512,1024]{1,0:T(8,128)S(1)}, s32[]{:T(128)}, s32[]{:T(128)}) while((s32[]{:T(128)}, f32[1024]{0:T(1024)S(1)}, f32[1024]{0:T(1024)S(1)}, f32[1024]{0:T(1024)S(1)}, f32[1024]{0:T(1024)S(1)}, ...), condition=%wide.region_5.6_spmd.clone, body=%wide.region_3.5_spmd.clone.sunk | while | flops 1582083 | bytes 2154591 | solution.py:44
  29.6 0.3 maximum_reduce_fusion.6
  29.9 0.3 maximum_reduce_fusion.6
  30.2 0.3 maximum_reduce_fusion.6
  30.5 0.3 maximum_reduce_fusion.6
  30.8 0.3 maximum_reduce_fusion.6
  31.2 0.3 maximum_reduce_fusion.6
  31.5 7.0 %fusion.27 = (f32[1024]{0:T(1024)S(1)}, f32[512,1024]{1,0:T(8,128)S(1)}, f32[1024,512]{0,1:T(8,128)}) fusion(f32[512,1024]{1,0:T(8,128)S(1)} %get-tuple-element.310, f32[1024]{0:T(1024)S(1)} %divide_add_fusion.1, f32[512,512]{1,0:T(8,128)S(1)} %copy-done, f32[512,1024]{1,0:T(8,128)} %copy-done.2), kind=kOutput, calls=%fused_computation.53 | convolution fusion | flops 3226991616 | bytes 9445376 | tf_op jit(solution)/shard_map/dot_general | solution.py:69
  38.5 0.0 copy-start.1
  38.5 0.3 maximum_reduce_fusion.2
  38.8 1.0 copy-done.1
  39.8 11.3 %while.35 = (s32[]{:T(128)}, f32[1024]{0:T(1024)S(1)}, f32[1024]{0:T(1024)S(1)}, f32[1024]{0:T(1024)S(1)}, f32[1024]{0:T(1024)S(1)}, /*index=5*/f32[512,1024]{1,0:T(8,128)}, s32[]{:T(128)}, s32[]{:T(128)}) while((s32[]{:T(128)}, f32[1024]{0:T(1024)S(1)}, f32[1024]{0:T(1024)S(1)}, f32[1024]{0:T(1024)S(1)}, f32[1024]{0:T(1024)S(1)}, ...), condition=%wide.region_11.12_spmd.clone, body=%wide.region_9.0_spmd.clone.sunk | while | flops 1582083 | bytes 2154591 | solution.py:44
  39.8 1.8 %maximum_reduce_fusion.7 = f32[1024]{0:T(1024)S(1)} fusion(f32[512,1024]{1,0:T(8,128)} %get-tuple-element.307, f32[1024]{0:T(1024)S(1)} %add_multiply_fusion.7), kind=kLoop, calls=%fused_computation.7.clone.1 | loop fusion | flops 1571840 | bytes 2105344 | tf_op jit(solution)/shard_map/while/body/eval_jaxpr/reduce_sum | solution.py:27
  41.7 1.8 %maximum_reduce_fusion.7 = f32[1024]{0:T(1024)S(1)} fusion(f32[512,1024]{1,0:T(8,128)} %get-tuple-element.307, f32[1024]{0:T(1024)S(1)} %add_multiply_fusion.7), kind=kLoop, calls=%fused_computation.7.clone.1 | loop fusion | flops 1571840 | bytes 2105344 | tf_op jit(solution)/shard_map/while/body/eval_jaxpr/reduce_sum | solution.py:27
  43.6 1.8 %maximum_reduce_fusion.7 = f32[1024]{0:T(1024)S(1)} fusion(f32[512,1024]{1,0:T(8,128)} %get-tuple-element.307, f32[1024]{0:T(1024)S(1)} %add_multiply_fusion.7), kind=kLoop, calls=%fused_computation.7.clone.1 | loop fusion | flops 1571840 | bytes 2105344 | tf_op jit(solution)/shard_map/while/body/eval_jaxpr/reduce_sum | solution.py:27
  45.5 1.8 %maximum_reduce_fusion.7 = f32[1024]{0:T(1024)S(1)} fusion(f32[512,1024]{1,0:T(8,128)} %get-tuple-element.307, f32[1024]{0:T(1024)S(1)} %add_multiply_fusion.7), kind=kLoop, calls=%fused_computation.7.clone.1 | loop fusion | flops 1571840 | bytes 2105344 | tf_op jit(solution)/shard_map/while/body/eval_jaxpr/reduce_sum | solution.py:27
  47.3 1.8 %maximum_reduce_fusion.7 = f32[1024]{0:T(1024)S(1)} fusion(f32[512,1024]{1,0:T(8,128)} %get-tuple-element.307, f32[1024]{0:T(1024)S(1)} %add_multiply_fusion.7), kind=kLoop, calls=%fused_computation.7.clone.1 | loop fusion | flops 1571840 | bytes 2105344 | tf_op jit(solution)/shard_map/while/body/eval_jaxpr/reduce_sum | solution.py:27
  49.2 1.8 %maximum_reduce_fusion.7 = f32[1024]{0:T(1024)S(1)} fusion(f32[512,1024]{1,0:T(8,128)} %get-tuple-element.307, f32[1024]{0:T(1024)S(1)} %add_multiply_fusion.7), kind=kLoop, calls=%fused_computation.7.clone.1 | loop fusion | flops 1571840 | bytes 2105344 | tf_op jit(solution)/shard_map/while/body/eval_jaxpr/reduce_sum | solution.py:27
  51.1 7.0 %fusion.9 = (f32[]{:T(128)}, f32[]{:T(128)}, f32[]{:T(128)}, f32[]{:T(128)}, f32[512,1024]{1,0:T(8,128)}) fusion(f32[1024,512]{0,1:T(8,128)} %get-tuple-element.168, f32[512,1024]{1,0:T(8,128)S(1)} %get-tuple-element.310, f32[1024]{0:T(1024)S(1)} %divide_add_fusion.1, f32[512,1024]{1,0:T(8,128)} %param.12, f32[1024,512]{0,1:T(8,128)} %get-tuple-element.169, ...), kind=kLoop, calls=%fused_computation.21 | loop fusion | flops 8388604 | bytes 12591120 | tf_op jit(solution)/shard_map/reduce_sum | solution.py:76
  58.1 2.6 %maximum_bitcast_fusion = (f32[1,2]{1,0:T(1,128)S(1)}, f32[1,2]{1,0:T(1,128)S(1)}) fusion(f32[1]{0:T(128)} %bitcast.5, f32[1]{0:T(128)} %bitcast.4, f32[1]{0:T(128)} %bitcast.8, f32[1]{0:T(128)} %bitcast.7), kind=kLoop, calls=%fused_computation.48 | loop fusion | flops 4 | bytes 32 | tf_op jit(solution)/shard_map/stack | solution.py:81
  60.7 8.0 %psum.28 = f32[2,2]{1,0:T(2,128)S(1)} all-reduce(f32[2,2]{1,0:T(2,128)S(1)} %pad_maximum_fusion), channel_id=1, replica_groups=mesh['pix_0'=4,'pix_1'=8,'pix_2'=2,'band'=4] {'pix_0'}, use_global_device_ids=true, to_apply=%region_16.17 | all-reduce | flops 4 | bytes 32 | tf_op jit(solution)/shard_map/psum | solution.py:17
  68.8 16.2 %psum.29 = f32[2,2]{1,0:T(2,128)S(1)} all-reduce(f32[2,2]{1,0:T(2,128)S(1)} %psum.28), channel_id=1, replica_groups=mesh['pix_0'=4,'pix_1'=8,'pix_2'=2,'band'=4] {'pix_1'}, use_global_device_ids=true, to_apply=%region_17.18 | all-reduce | flops 4 | bytes 32 | tf_op jit(solution)/shard_map/psum | solution.py:17
  85.0 12.4 %psum.30 = f32[2,2]{1,0:T(2,128)S(1)} all-reduce(f32[2,2]{1,0:T(2,128)S(1)} %psum.29), channel_id=1, replica_groups=mesh['pix_0'=4,'pix_1'=8,'pix_2'=2,'band'=4] {'pix_2'}, use_global_device_ids=true, to_apply=%region_18.19 | all-reduce | flops 4 | bytes 32 | tf_op jit(solution)/shard_map/psum | solution.py:17
  97.4 7.1 %psum.31 = f32[2,2]{1,0:T(2,128)S(1)} all-reduce(f32[2,2]{1,0:T(2,128)S(1)} %psum.30), channel_id=1, replica_groups=mesh['pix_0'=4,'pix_1'=8,'pix_2'=2,'band'=4] {'band'}, use_global_device_ids=true, to_apply=%region_19.20 | all-reduce | flops 4 | bytes 32 | tf_op jit(solution)/shard_map/psum | solution.py:17
  104.5 0.6 multiply_sqrt_fusion
  105.1 4.1 %sub.115 = f32[512,1024]{1,0:T(8,128)} subtract(f32[512,1024]{1,0:T(8,128)} %get-tuple-element.311, f32[512,1024]{1,0:T(8,128)} %get-tuple-element.155) | non-fusion elementwise | flops 524288 | bytes 6291456 | tf_op jit(solution)/shard_map/sub | solution.py:75
  (31 shorter events, 0.2 us)
Async XLA Ops:
  0.6 19.9 %copy-start = (f32[512,512]{1,0:T(8,128)S(1)}, f32[512,512]{1,0:T(8,128)}, u32[]{:S(2)}) copy-start(f32[512,512]{1,0:T(8,128)} %param.11) | copy-start | bytes 3145732
  2.5 17.5 %all-to-all-start = ((bf16[56,4,1024]{2,0,1:T(8,128)(2,1)}), bf16[56,4,1024]{2,0,1:T(8,128)(2,1)S(1)}, u32[]{:S(2)}, u32[]{:S(2)}) async-start(bf16[56,4,1024]{2,0,1:T(8,128)(2,1)} %bitcast.34), calls=%async_computation | async-start | bytes 917504 | tf_op jit(solution)/shard_map/all_to_all | solution.py:59
  20.5 8.7 %copy-start.2 = (f32[512,1024]{1,0:T(8,128)}, f32[512,1024]{1,0:T(8,128)S(1)}, u32[]{:S(2)}) copy-start(f32[512,1024]{1,0:T(8,128)S(1)} %fusion.29) | copy-start | bytes 6291460
  38.5 1.4 %copy-start.1 = (f32[512,1024]{1,0:T(8,128)}, f32[512,1024]{1,0:T(8,128)S(1)}, u32[]{:S(2)}) copy-start(f32[512,1024]{1,0:T(8,128)S(1)} %get-tuple-element.291) | copy-start | bytes 6291460
where the time goes:
time: 110 us; the launch traced here: 109 us
  blocking collectives  56.2 us (51%)
  other arithmetic  27.9 us (25%)
  matrix products  16.1 us (15%)
  starting transfers between devices  5 us (5%)
  local copies, waits for them, and re-layouts  2.93 us (3%)
    psum x4, blocking collectives, one_axis_at_a_time(): shard = lax.psum(shard, axis)  43.7 us
    dot_general x2, matrix products, body(): jnp.dot(gram_inverse, fit_term / penalty + current - scaled_dual, precisi...  15.7 us
    reduce_sum x14, other arithmetic, mass_at(): return jnp.sum(jnp.maximum(shifted - level[None, :], 0.0), axis=0)  13.3 us
    all_gather x1, blocking collectives, body(): all_rows = lax.all_gather(endmembers, 'band', axis=0, tiled=True)  12.5 us
    reduce_sum x1, other arithmetic, body(): primal_sum = jnp.sum((primal - updated) ** 2)  7.01 us
    all_to_all x1, starting transfers between devices, body(): lax.all_to_all(spectra, 'band', split_axis=1, concat_axis=0, tiled=True)  5 us
    sub x1, other arithmetic, body(): scaled_dual = scaled_dual + primal - updated  4.1 us
    another operation x2, other arithmetic, body(): totals = jnp.stack([jnp.stack(primal_list), jnp.stack(change_list)])  2.64 us
  transfers between devices with their start and end apart: 1, of which 0 were waited for; matrix products, arithmetic and copies ran while one was open for 0% of the time, Pallas kernels for 0%

commit v1 on v0

--- a/solution.py
+++ b/solution.py
@@ -10,6 +10,29 @@
 BISECT = 6
 PIX = ("pix_0", "pix_1", "pix_2")
 PIX_BAND = ("pix_0", "pix_1", "pix_2", "band")
+
+
+def cut_along(x, dim, devices):
+    shape = x.shape
+    pieces = x.reshape(*shape[:dim], devices, shape[dim] // devices, *shape[dim + 1 :])
+    return jnp.moveaxis(pieces, dim, 0)
+
+
+def joined_along(tiles, dim):
+    tiles = jnp.moveaxis(tiles, 0, dim)
+    dims = tiles.shape
+    return tiles.reshape(*dims[:dim], dims[dim] * dims[dim + 1], *dims[dim + 2 :])
+
+
+def pairwise_exchange(x, axis, split_dim, concat_dim):
+    size, index = (lax.axis_size(axis), lax.axis_index(axis))
+    blocks = cut_along(x, split_dim, size)
+    outs = [blocks[index]]
+    for lap in range(1, size):
+        sent = blocks[index ^ lap]
+        outs.append(lax.ppermute(sent, axis, [(i, i ^ lap) for i in range(size)]))
+    blocks = jnp.stack(outs)[index ^ jnp.arange(size)]
+    return joined_along(blocks, concat_dim)
 
 
 def one_axis_at_a_time(shard, axes):
@@ -56,7 +79,7 @@
 
 def body(spectra, endmembers, gram_inverse, abundances, duals):
     penalty = B / (2.0 * K * K)
-    exchanged = lax.all_to_all(spectra, "band", split_axis=1, concat_axis=0, tiled=True)
+    exchanged = pairwise_exchange(spectra, "band", 1, 0)
     all_rows = lax.all_gather(endmembers, "band", axis=0, tiled=True)
     fit_term = contract_bands(all_rows, exchanged)
     fit_term = fit_term / K

time: 110 us -> 118 us (1.073)
  local copies, waits for them, and re-layouts: 2.93 us -> 21 us
  other arithmetic: 27.9 us -> 19.3 us
    unnamed x6 -> x20, local copies, waits for them, and re-layouts: 1.02 us -> 16.3 us
    reduce_sum x14, other arithmetic: 13.3 us -> 7.65 us  [mass_at(): return jnp.sum(jnp.maximum(shifted - level[None, :], 0.0), axis=0)]
    all_to_all x1 -> x0, starting transfers between devices: 5 us -> none  [body(): lax.all_to_all(spectra, 'band', split_axis=1, concat_axis=0, tiled=True)]
    ppermute x0 -> x3, starting transfers between devices: none -> 4.74 us  [pairwise_exchange(): outs.append(lax.ppermute(sent, axis, [(i, i ^ lap) for i in range(size)]))]
    sub x1 -> x0, other arithmetic: 4.1 us -> none  [body(): scaled_dual = scaled_dual + primal - updated]
    gather x0 -> x1, local copies, waits for them, and re-layouts: none -> 2.36 us  [pairwise_exchange(): blocks = jnp.stack(outs)[index ^ jnp.arange(size)]]
    all_to_all x1 -> x0, local copies, waits for them, and re-layouts: 1.9 us -> none  [body(): lax.all_to_all(spectra, 'band', split_axis=1, concat_axis=0, tiled=True)]
    another operation x0 -> x1, other arithmetic: none -> 1.84 us  [pairwise_exchange(): blocks = jnp.stack(outs)[index ^ jnp.arange(size)]]
  transfers between devices with their start and end apart: 1 -> 3, of which waited for: 0 -> 0; matrix products, arithmetic and copies ran while one was open for 0% -> 6% of each run, Pallas kernels for 0% -> 0%
where the time goes in v1:
time: 118 us; the launch traced here: 117 us
  blocking collectives  55.1 us (47%)
  local copies, waits for them, and re-layouts  21 us (18%)
  other arithmetic  19.3 us (16%)
  matrix products  15.7 us (13%)
  starting transfers between devices  4.74 us (4%)
    psum x4, blocking collectives, one_axis_at_a_time(): shard = lax.psum(shard, axis)  43 us
    unnamed x20, local copies, waits for them, and re-layouts  16.3 us
    dot_general x2, matrix products, body(): jnp.dot(gram_inverse, fit_term / penalty + current - scaled_dual, precisi...  14.1 us
    all_gather x1, blocking collectives, body(): all_rows = lax.all_gather(endmembers, 'band', axis=0, tiled=True)  12.1 us
    reduce_sum x14, other arithmetic, mass_at(): return jnp.sum(jnp.maximum(shifted - level[None, :], 0.0), axis=0)  7.65 us
    reduce_sum x1, other arithmetic, body(): primal_sum = jnp.sum((primal - updated) ** 2)  6.42 us
    ppermute x3, starting transfers between devices, pairwise_exchange(): outs.append(lax.ppermute(sent, axis, [(i, i ^ lap) for i in range(size)]))  4.74 us
    another operation x2, other arithmetic, body(): totals = jnp.stack([jnp.stack(primal_list), jnp.stack(change_list)])  2.57 us
  transfers between devices with their start and end apart: 3, of which 0 were waited for; matrix products, arithmetic and copies ran while one was open for 6% of the time, Pallas kernels for 0%

profile of v1, /device:TPU:1, one launch (start us, length us, event | category | flops | bytes accessed | tf_op | source)
XLA Modules:
  0.0 117.0 jit_solution(10070453341550499028)
XLA Ops:
  0.6 0.0 copy-start
  0.7 1.4 %reshape.47 = bf16[56,4,1024]{2,1,0:T(4,128)(2,1)S(1)} reshape(bf16[56,4096]{1,0:T(8,128)(2,1)} %param.9) | data formatting | bytes 917504 | tf_op jit(solution)/shard_map/reshape | solution.py:17
  2.1 1.0 constant_dynamic-slice_fusion.3
  3.1 0.7 copy.50
  3.8 2.1 %collective-permute-start = (bf16[56,1024]{1,0:T(8,128)(2,1)}, bf16[56,1024]{1,0:T(8,128)(2,1)}, u32[]{:S(2)}, u32[]{:S(2)}) collective-permute-start(bf16[56,1024]{1,0:T(8,128)(2,1)} %bitcast.57), channel_id=1, source_target_pairs={{0,1},{1,0},{2,3},{3,2},{4,5},{5,4},{6,7},{7,6},{8,9},{9,8},{10,11... | collective-permute-start | bytes 344072 | tf_op jit(solution)/shard_map/ppermute | solution.py:33
  5.9 0.7 copy.49
  6.6 2.6 %collective-permute-start.1 = (bf16[56,1024]{1,0:T(8,128)(2,1)}, bf16[56,1024]{1,0:T(8,128)(2,1)}, u32[]{:S(2)}, u32[]{:S(2)}) collective-permute-start(bf16[56,1024]{1,0:T(8,128)(2,1)} %bitcast.56), channel_id=1, source_target_pairs={{0,2},{1,3},{2,0},{3,1},{4,6},{5,7},{6,4},{7,5},{8,10},{9,11},{10,... | collective-permute-start | bytes 344072 | tf_op jit(solution)/shard_map/ppermute | solution.py:33
  9.2 0.7 copy.48
  9.9 0.0 collective-permute-start.2
  9.9 12.1 %all_gather.3 = bf16[224,512]{1,0:T(8,128)(2,1)S(1)} all-gather(bf16[56,512]{1,0:T(8,128)(2,1)S(1)} %copy-done.4), channel_id=1, replica_groups=mesh['pix_0'=4,'pix_1'=8,'pix_2'=2,'band'=4] {'band'}, dimensions={0}, use_global_device_ids=true | all-gather | bytes 286720 | tf_op jit(solution)/shard_map/all_gather | solution.py:83
  22.0 1.9 %copy.28 = f32[512,1024]{0,1:T(8,128)S(1)} copy(f32[512,1024]{1,0:T(8,128)} %param.12) | data formatting | bytes 4194304 | tf_op args[3]
  23.9 3.6 %copy.29 = f32[512,1024]{0,1:T(8,128)} copy(f32[512,1024]{1,0:T(8,128)} %param.13) | data formatting | bytes 4194304 | tf_op args[4]
  27.6 0.0 collective-permute-done
  27.6 0.0 collective-permute-done.1
  27.6 0.0 collective-permute-done.2
  27.6 1.8 %pad_maximum_fusion = bf16[4,56,1024]{2,1,0:T(8,128)(2,1)} fusion(bf16[1,56,1024]{2,1,0:T(8,128)(2,1)} %bitcast.2, bf16[1,56,1024]{2,1,0:T(8,128)(2,1)} %bitcast.1, bf16[1,56,1024]{2,1,0:T(8,128)(2,1)} %bitcast, bf16[1,56,1024]{2,1,0:T(8,128)(2,1)S(1)} %bitcast.60), kind=kLoop, calls=%fused_computation.42 | loop fusion | flops 688128 | bytes 917504 | tf_op jit(solution)/shard_map/stack | solution.py:34
  29.5 2.4 %gather_fusion = bf16[4,56,1024]{2,1,0:T(8,128)(2,1)} fusion(bf16[4,56,1024]{2,1,0:T(8,128)(2,1)} %pad_maximum_fusion, s32[1024]{0:T(1024)S(1)} %pad_clamp_fusion), kind=kCustom, calls=%fused_computation | custom fusion | bytes 917520 | tf_op jit(solution)/shard_map/gather | solution.py:34
  31.8 1.6 %fusion.31 = f32[1024,512]{1,0:T(8,128)S(1)} fusion(bf16[224,1024]{1,0:T(8,128)(2,1)} %bitcast.59, bf16[224,512]{1,0:T(8,128)(2,1)S(1)} %all_gather.3), kind=kOutput, calls=%fused_computation.68 | convolution fusion | flops 234881024 | bytes 2785280 | tf_op jit(solution)/shard_map/dot_general | solution.py:75
  33.5 0.1 copy-done.3
  33.6 5.2 %fusion.30 = (f32[1024]{0:T(1024)S(1)}, f32[512,1024]{0,1:T(8,128)}, f32[1024,512]{1,0:T(8,128)}) fusion(f32[512,1024]{0,1:T(8,128)S(1)} %copy-done.3, f32[512,512]{1,0:T(8,128)S(1)} %copy-done, f32[512,1024]{0,1:T(8,128)S(1)} %copy.28, f32[1024,512]{1,0:T(8,128)S(1)} %fusion.31), kind=kOutput, calls=%fused_computation.67 | convolution fusion | flops 3223845888 | bytes 11538432 | tf_op jit(solution)/shard_map/dot_general | solution.py:92
  38.8 1.9 %copy.32 = f32[512,1024]{1,0:T(8,128)S(1)} copy(f32[512,1024]{0,1:T(8,128)} %get-tuple-element.203) | data formatting | bytes 4194304
  40.7 2.2 %maximum_reduce_fusion.3 = (f32[1024]{0:T(1024)S(1)}, f32[1024]{0:T(1024)S(1)}) fusion(f32[512,1024]{0,1:T(8,128)} %get-tuple-element.203, f32[1024]{0:T(1024)S(1)} %add_multiply_fusion.3), kind=kLoop, calls=%fused_computation.35 | loop fusion | flops 2095104 | bytes 2109440 | tf_op jit(solution)/shard_map/reduce_sum | solution.py:50
  42.9 1.9 %while.34 = (s32[]{:T(128)}, f32[1024]{0:T(1024)S(1)}, f32[1024]{0:T(1024)S(1)}, f32[1024]{0:T(1024)S(1)}, f32[1024]{0:T(1024)S(1)}, /*index=5*/f32[512,1024]{1,0:T(8,128)S(1)}, s32[]{:T(128)}, s32[]{:T(128)}) while((s32[]{:T(128)}, f32[1024]{0:T(1024)S(1)}, f32[1024]{0:T(1024)S(1)}, f32[1024]{0:T(1024)S(1)}, f32[1024]{0:T(1024)S(1)}, ...), condition=%wide.region_5.6_spmd.clone, body=%wide.region_3.5_spmd.clone.sunk | while | flops 1582083 | bytes 2154591 | solution.py:67
  42.9 0.3 maximum_reduce_fusion.6
  43.3 0.3 maximum_reduce_fusion.6
  43.6 0.3 maximum_reduce_fusion.6
  43.9 0.3 maximum_reduce_fusion.6
  44.2 0.3 maximum_reduce_fusion.6
  44.5 0.3 maximum_reduce_fusion.6
  44.8 8.9 %fusion.29 = (f32[1024]{0:T(1024)S(1)}, f32[512,1024]{0,1:T(8,128)}, f32[1024,512]{1,0:T(8,128)}) fusion(f32[512,1024]{0,1:T(8,128)} %get-tuple-element.203, f32[1024]{0:T(1024)S(1)} %divide_add_fusion.1, f32[512,512]{1,0:T(8,128)S(1)} %copy-done, f32[1024,512]{1,0:T(8,128)} %copy-done.2), kind=kOutput, calls=%fused_computation.66 | convolution fusion | flops 3226991616 | bytes 9445376 | tf_op jit(solution)/shard_map/dot_general | solution.py:92
  53.7 1.9 %copy.34 = f32[512,1024]{1,0:T(8,128)S(1)} copy(f32[512,1024]{0,1:T(8,128)} %get-tuple-element.201) | data formatting | bytes 4194304
  55.6 2.2 %maximum_reduce_fusion.2 = (f32[1024]{0:T(1024)S(1)}, f32[1024]{0:T(1024)S(1)}) fusion(f32[512,1024]{0,1:T(8,128)} %get-tuple-element.201, f32[1024]{0:T(1024)S(1)} %add_multiply_fusion.2), kind=kLoop, calls=%fused_computation.32 | loop fusion | flops 2095104 | bytes 2109440 | tf_op jit(solution)/shard_map/reduce_sum | solution.py:50
  57.8 1.9 %while.35 = (s32[]{:T(128)}, f32[1024]{0:T(1024)S(1)}, f32[1024]{0:T(1024)S(1)}, f32[1024]{0:T(1024)S(1)}, f32[1024]{0:T(1024)S(1)}, /*index=5*/f32[512,1024]{1,0:T(8,128)S(1)}, s32[]{:T(128)}, s32[]{:T(128)}) while((s32[]{:T(128)}, f32[1024]{0:T(1024)S(1)}, f32[1024]{0:T(1024)S(1)}, f32[1024]{0:T(1024)S(1)}, ...), condition=%wide.region_11.12_spmd.clone, body=%wide.region_9.0_spmd.clone.sunk | while | flops 1582083 | bytes 2154591 | solution.py:67
  57.8 0.3 maximum_reduce_fusion.7
  58.1 0.3 maximum_reduce_fusion.7
  58.5 0.3 maximum_reduce_fusion.7
  58.8 0.3 maximum_reduce_fusion.7
  59.1 0.3 maximum_reduce_fusion.7
  59.4 0.3 maximum_reduce_fusion.7
  59.7 6.4 %fusion.9 = (f32[]{:T(128)}, f32[]{:T(128)}, f32[]{:T(128)}, f32[]{:T(128)}, f32[512,1024]{0,1:T(8,128)}, /*index=5*/f32[512,1024]{0,1:T(8,128)S(1)}) fusion(f32[1024,512]{1,0:T(8,128)} %get-tuple-element.218, f32[512,1024]{0,1:T(8,128)} %get-tuple-element.203, f32[1024]{0:T(1024)S(1)} %divide_add_fusion.1, f32[512,1024]{0,1:T(8,128)} %copy-done.1, ...), kind=kLoop, calls=%fused_computation.22 | loop fusion | flops 8912892 | bytes 14688272 | tf_op jit(solution)/shard_map/reduce_sum | solution.py:99
  66.1 2.6 %maximum_bitcast_fusion = (f32[1,2]{1,0:T(1,128)S(1)}, f32[1,2]{1,0:T(1,128)S(1)}) fusion(f32[1]{0:T(128)} %bitcast.9, f32[1]{0:T(128)} %bitcast.8, f32[1]{0:T(128)} %bitcast.12, f32[1]{0:T(128)} %bitcast.11), kind=kLoop, calls=%fused_computation.60 | loop fusion | flops 4 | bytes 32 | tf_op jit(solution)/shard_map/stack | solution.py:104
  68.7 8.5 %psum.28 = f32[2,2]{1,0:T(2,128)S(1)} all-reduce(f32[2,2]{1,0:T(2,128)S(1)} %pad_maximum_fusion.1), channel_id=1, replica_groups=mesh['pix_0'=4,'pix_1'=8,'pix_2'=2,'band'=4] {'pix_0'}, use_global_device_ids=true, to_apply=%region_16.17 | all-reduce | flops 4 | bytes 32 | tf_op jit(solution)/shard_map/psum | solution.py:40
  77.2 16.2 %psum.29 = f32[2,2]{1,0:T(2,128)S(1)} all-reduce(f32[2,2]{1,0:T(2,128)S(1)} %psum.28), channel_id=1, replica_groups=mesh['pix_0'=4,'pix_1'=8,'pix_2'=2,'band'=4] {'pix_1'}, use_global_device_ids=true, to_apply=%region_17.18 | all-reduce | flops 4 | bytes 32 | tf_op jit(solution)/shard_map/psum | solution.py:40
  93.4 10.8 %psum.30 = f32[2,2]{1,0:T(2,128)S(1)} all-reduce(f32[2,2]{1,0:T(2,128)S(1)} %psum.29), channel_id=1, replica_groups=mesh['pix_0'=4,'pix_1'=8,'pix_2'=2,'band'=4] {'pix_2'}, use_global_device_ids=true, to_apply=%region_18.19 | all-reduce | flops 4 | bytes 32 | tf_op jit(solution)/shard_map/psum | solution.py:40
  104.2 2.9 %copy.36 = f32[512,1024]{1,0:T(8,128)} copy(f32[512,1024]{0,1:T(8,128)} %get-tuple-element.212) | data formatting | bytes 4194304
  107.1 7.6 %psum.31 = f32[2,2]{1,0:T(2,128)S(1)} all-reduce(f32[2,2]{1,0:T(2,128)S(1)} %psum.30), channel_id=1, replica_groups=mesh['pix_0'=4,'pix_1'=8,'pix_2'=2,'band'=4] {'band'}, use_global_device_ids=true, to_apply=%region_19.20 | all-reduce | flops 4 | bytes 32 | tf_op jit(solution)/shard_map/psum | solution.py:40
  114.6 0.6 multiply_sqrt_fusion
  115.2 1.8 %copy.37 = f32[512,1024]{1,0:T(8,128)} copy(f32[512,1024]{0,1:T(8,128)S(1)} %get-tuple-element.213) | data formatting | bytes 4194304
  (42 shorter events, 0.3 us)
Async XLA Ops:
  0.6 32.8 %copy-start = (f32[512,512]{1,0:T(8,128)S(1)}, f32[512,512]{1,0:T(8,128)}, u32[]{:S(2)}) copy-start(f32[512,512]{1,0:T(8,128)} %param.11) | copy-start | bytes 3145732
  0.6 9.2 %copy-start.4 = (bf16[56,512]{1,0:T(8,128)(2,1)S(1)}, bf16[56,512]{1,0:T(8,128)(2,1)}, u32[]{:S(2)}) copy-start(bf16[56,512]{1,0:T(8,128)(2,1)} %param.10) | copy-start | bytes 172036
  3.8 23.8 %collective-permute-start = (bf16[56,1024]{1,0:T(8,128)(2,1)}, bf16[56,1024]{1,0:T(8,128)(2,1)}, u32[]{:S(2)}, u32[]{:S(2)}) collective-permute-start(bf16[56,1024]{1,0:T(8,128)(2,1)} %bitcast.57), channel_id=1, source_target_pairs={{0,1},{1,0},{2,3},{3,2},{4,5},{5,4},{6,7},{7,6},{8,9},{9,8},{10,11... | collective-permute-start | bytes 344072 | tf_op jit(solution)/shard_map/ppermute | solution.py:33
  6.6 21.0 %collective-permute-start.1 = (bf16[56,1024]{1,0:T(8,128)(2,1)}, bf16[56,1024]{1,0:T(8,128)(2,1)}, u32[]{:S(2)}, u32[]{:S(2)}) collective-permute-start(bf16[56,1024]{1,0:T(8,128)(2,1)} %bitcast.56), channel_id=1, source_target_pairs={{0,2},{1,3},{2,0},{3,1},{4,6},{5,7},{6,4},{7,5},{8,10},{9,11},{10,... | collective-permute-start | bytes 344072 | tf_op jit(solution)/shard_map/ppermute | solution.py:33
  9.9 17.7 %collective-permute-start.2 = (bf16[56,1024]{1,0:T(8,128)(2,1)}, bf16[56,1024]{1,0:T(8,128)(2,1)}, u32[]{:S(2)}, u32[]{:S(2)}) collective-permute-start(bf16[56,1024]{1,0:T(8,128)(2,1)} %bitcast.55), channel_id=1, source_target_pairs={{0,3},{1,2},{2,1},{3,0},{4,7},{5,6},{6,5},{7,4},{8,11},{9,10},{10,... | collective-permute-start | bytes 344072 | tf_op jit(solution)/shard_map/ppermute | solution.py:33
  23.9 9.5 %copy-start.1 = (f32[512,1024]{0,1:T(8,128)}, f32[512,1024]{0,1:T(8,128)S(1)}, u32[]{:S(2)}) copy-start(f32[512,1024]{0,1:T(8,128)S(1)} %copy.28) | copy-start | bytes 6291460
  31.8 1.7 %copy-start.3 = (f32[512,1024]{0,1:T(8,128)S(1)}, f32[512,1024]{0,1:T(8,128)}, u32[]{:S(2)}) copy-start(f32[512,1024]{0,1:T(8,128)} %copy.29) | copy-start | bytes 6291460
  33.5 5.3 %copy-start.2 = (f32[1024,512]{1,0:T(8,128)}, f32[1024,512]{1,0:T(8,128)S(1)}, u32[]{:S(2)}) copy-start(f32[1024,512]{1,0:T(8,128)S(1)} %fusion.31) | copy-start | bytes 6291460
